TPU v7x, 32 devices: a whole 2x2x4 slice. The times are simulated.
32 devices in a mesh: seq: 4 (over y, x), ctx: 8 (over z, core).
Axes of the slice: x: 2, y: 2, z: 4, core: 2. Of those that a mesh axis runs over, the one named last changes fastest.
Arguments:
- inputs: bfloat16 [4096, 1152], P(('seq', 'ctx')), may hold values from -140 to 140
- positions: int32 [4096], P(('seq', 'ctx')), may hold values from 0 to 1023, as said below
- attention_gain: bfloat16 [1152], P(('seq', 'ctx')), may hold values from 0.3984375 to 1.59375
- query_weight: bfloat16 [1152, 1024], P(('seq', 'ctx')), may hold values from -0.1875 to 0.1875
- key_weight: bfloat16 [1152, 256], P(('seq', 'ctx')), may hold values from -0.1875 to 0.1875
- value_weight: bfloat16 [1152, 256], P(('seq', 'ctx')), may hold values from -0.1875 to 0.1875
- query_gain: bfloat16 [256], P(('seq', 'ctx')), may hold values from 0.5 to 1.5
- key_gain: bfloat16 [256], P(('seq', 'ctx')), may hold values from 0.5 to 1.5
- output_weight: bfloat16 [1024, 1152], P(('seq', 'ctx')), may hold values from -0.1875 to 0.1875
- attention_post: bfloat16 [1152], P(('seq', 'ctx')), may hold values from 0.3984375 to 1.59375
- feedfwd_gain: bfloat16 [1152], P(('seq', 'ctx')), may hold values from 0.3984375 to 1.59375
- gate_weight: bfloat16 [1152, 6912], P(('seq', 'ctx')), may hold values from -0.1875 to 0.1875
- up_weight: bfloat16 [1152, 6912], P(('seq', 'ctx')), may hold values from -0.1875 to 0.1875
- down_weight: bfloat16 [6912, 1152], P(('seq', 'ctx')), may hold values from -0.078125 to 0.078125
- feedfwd_post: bfloat16 [1152], P(('seq', 'ctx')), may hold values from 0.3984375 to 1.59375
- cotangent: bfloat16 [4096, 1152], P(('seq', 'ctx')), may hold values from -6 to 6
Outputs:
- block_out: bfloat16 [4096, 1152], P(('seq', 'ctx'))
- input_grad: float32 [4096, 1152], P(('seq', 'ctx'))
- attention_gain_grad: float32 [1152], P(('seq', 'ctx'))
- query_grad: float32 [1152, 1024], P(('seq', 'ctx'))
- key_grad: float32 [1152, 256], P(('seq', 'ctx'))
- value_grad: float32 [1152, 256], P(('seq', 'ctx'))
- query_gain_grad: float32 [256], P(('seq', 'ctx'))
- key_gain_grad: float32 [256], P(('seq', 'ctx'))
- output_grad: float32 [1024, 1152], P(('seq', 'ctx'))
- attention_post_grad: float32 [1152], P(('seq', 'ctx'))
- feedfwd_gain_grad: float32 [1152], P(('seq', 'ctx'))
- gate_grad: float32 [1152, 6912], P(('seq', 'ctx'))
- up_grad: float32 [1152, 6912], P(('seq', 'ctx'))
- down_grad: float32 [6912, 1152], P(('seq', 'ctx'))
- feedfwd_post_grad: float32 [1152], P(('seq', 'ctx'))
Inputs may be any that keep to these rules, and one draw needn't show every extreme that they name: Within each sequence of 1024 tokens, the 128 tokens of each ctx index hold the consecutive positions k * 128 to k * 128 + 127, where the block numbers k of one sequence's ctx indices are a permutation of 0 to 7, drawn afresh for every sequence.
All inputs are finite; a program needn't handle non-finite values.
Results may differ from a plain program's by a relative error of at most 0.038.
Values may be sent and summed in bfloat16 or wider, within the bound.
A program may use at most 448 MiB of HBM per device.

v0:
```python
import math
import jax
import jax.numpy as jnp
from jax import lax
from jax.sharding import PartitionSpec as P

D = 1152
H = 4
DH = 256
FF = 6912
EPSILON = 1e-06
THETA = 1000000.0
GELU_COEF = math.sqrt(2.0 / math.pi)


def rms_factor(values):
    return lax.rsqrt(jnp.mean(values * values, axis=-1, keepdims=True) + EPSILON)


def norm_back(values, factor, gain_vector, upstream):
    scaled = gain_vector * upstream
    cubed = factor * factor * factor
    return factor * scaled - values * cubed * jnp.mean(scaled * values, axis=-1, keepdims=True)


def rotary(places):
    half_width = DH // 2
    exponent = jnp.arange(half_width, dtype=jnp.float32) * (-2.0 / DH)
    frequency = jnp.power(jnp.float32(THETA), exponent)
    angles = places.astype(jnp.float32)[:, None] * frequency[None, :]
    return (jnp.cos(angles), jnp.sin(angles))


def rotate(values, cosine, sinus):
    half_width = values.shape[-1] // 2
    first = values[..., :half_width]
    second = values[..., half_width:]
    return jnp.concatenate(
        [first * cosine - second * sinus, second * cosine + first * sinus], axis=-1
    )


def rotate_back(upstream, cosine, sinus):
    half_width = upstream.shape[-1] // 2
    first = upstream[..., :half_width]
    second = upstream[..., half_width:]
    return jnp.concatenate(
        [first * cosine + second * sinus, second * cosine - first * sinus], axis=-1
    )


def gelu_tanh(values):
    inner = GELU_COEF * (values + 0.044715 * values * values * values)
    return 0.5 * values * (1.0 + jnp.tanh(inner))


def gelu_slope(values):
    inner = GELU_COEF * (values + 0.044715 * values * values * values)
    tangent = jnp.tanh(inner)
    return 0.5 * (1.0 + tangent) + 0.5 * values * (1.0 - tangent * tangent) * GELU_COEF * (
        1.0 + 3.0 * 0.044715 * values * values
    )


def times_right(left_side, right_side):
    return jnp.dot(left_side, right_side, preferred_element_type=jnp.float32)


def times_transposed(left_side, right_side):
    return lax.dot_general(
        left_side, right_side, (((1,), (1,)), ((), ())), preferred_element_type=jnp.float32
    )


def transposed_times(left_side, right_side):
    return lax.dot_general(
        left_side, right_side, (((0,), (0,)), ((), ())), preferred_element_type=jnp.float32
    )


def attend_back(
    query_part, place_part, output_part, logsum_part, upper_part, key_all, value_all, place_all
):
    scaling = 1.0 / math.sqrt(DH)
    upper_round = upper_part.astype(jnp.bfloat16)
    row_delta = jnp.sum(upper_part * output_part.astype(jnp.float32), axis=-1)
    scores = (
        jnp.einsum("qhd,kd->hqk", query_part, key_all, preferred_element_type=jnp.float32) * scaling
    )
    allowed = place_all[None, None, :] <= place_part[None, :, None]
    probability = jnp.where(allowed, jnp.exp(scores - jnp.transpose(logsum_part)[:, :, None]), 0.0)
    value_sum = jnp.einsum(
        "hqk,qhd->kd",
        probability.astype(jnp.bfloat16),
        upper_round,
        preferred_element_type=jnp.float32,
    )
    prob_back = jnp.einsum(
        "qhd,kd->hqk", upper_round, value_all, preferred_element_type=jnp.float32
    )
    score_back = (
        probability * (prob_back - jnp.transpose(row_delta)[:, :, None]) * scaling
    ).astype(jnp.bfloat16)
    query_back = jnp.einsum("hqk,kd->qhd", score_back, key_all, preferred_element_type=jnp.float32)
    key_back = jnp.einsum("hqk,qhd->kd", score_back, query_part, preferred_element_type=jnp.float32)
    return (query_back, key_back, value_sum)


def per_device(
    inputs,
    positions,
    attention_gain,
    query_weight,
    key_weight,
    value_weight,
    query_gain,
    key_gain,
    output_weight,
    attention_post,
    feedfwd_gain,
    gate_weight,
    up_weight,
    down_weight,
    feedfwd_post,
    cotangent,
):
    attention_set = (
        lax.all_gather(attention_gain, ("seq", "ctx"), axis=0, tiled=True),
        lax.all_gather(query_weight, ("seq", "ctx"), axis=0, tiled=True),
        lax.all_gather(key_weight, ("seq", "ctx"), axis=0, tiled=True),
        lax.all_gather(value_weight, ("seq", "ctx"), axis=0, tiled=True),
        lax.all_gather(query_gain, ("seq", "ctx"), axis=0, tiled=True),
        lax.all_gather(key_gain, ("seq", "ctx"), axis=0, tiled=True),
        lax.all_gather(output_weight, ("seq", "ctx"), axis=0, tiled=True),
        lax.all_gather(attention_post, ("seq", "ctx"), axis=0, tiled=True),
    )
    feedfwd_set = (
        lax.all_gather(feedfwd_gain, ("seq", "ctx"), axis=0, tiled=True),
        lax.all_gather(gate_weight, ("seq", "ctx"), axis=0, tiled=True),
        lax.all_gather(up_weight, ("seq", "ctx"), axis=0, tiled=True),
        lax.all_gather(down_weight, ("seq", "ctx"), axis=0, tiled=True),
        lax.all_gather(feedfwd_post, ("seq", "ctx"), axis=0, tiled=True),
    )
    gain_attention = attention_set[0].astype(jnp.float32)
    gain_query = attention_set[4].astype(jnp.float32)
    gain_key = attention_set[5].astype(jnp.float32)
    gain_post = attention_set[7].astype(jnp.float32)
    gain_feed = feedfwd_set[0].astype(jnp.float32)
    gain_final = feedfwd_set[4].astype(jnp.float32)
    token_count = inputs.shape[0]
    scaling = 1.0 / math.sqrt(DH)
    device_total = lax.axis_size(("seq", "ctx"))
    input_wide = inputs.astype(jnp.float32)
    input_factor = rms_factor(input_wide)
    normed = (input_wide * input_factor * gain_attention).astype(jnp.bfloat16)
    queries = times_right(normed, attention_set[1]).reshape(token_count, H, DH)
    key_rows = times_right(normed, attention_set[2])
    value_rows = times_right(normed, attention_set[3]).astype(jnp.bfloat16)
    cosine, sinus = rotary(positions)
    query_factor = rms_factor(queries)
    query_rot = rotate(
        queries * query_factor * gain_query, cosine[:, None, :], sinus[:, None, :]
    ).astype(jnp.bfloat16)
    key_factor = rms_factor(key_rows)
    key_rot = rotate(key_rows * key_factor * gain_key, cosine, sinus).astype(jnp.bfloat16)
    key_piece = lax.all_gather(key_rot, "ctx", axis=0, tiled=True)
    value_piece = lax.all_gather(value_rows, "ctx", axis=0, tiled=True)
    place_piece = lax.all_gather(positions, "ctx", axis=0, tiled=True)
    scores = (
        jnp.einsum("qhd,kd->hqk", query_rot, key_piece, preferred_element_type=jnp.float32)
        * scaling
    )
    allowed = place_piece[None, None, :] <= positions[None, :, None]
    expscore = jnp.where(allowed, jnp.exp(scores), 0.0)
    weight_sum = jnp.sum(expscore, axis=-1)
    summed = jnp.einsum(
        "hqk,kd->qhd",
        expscore.astype(jnp.bfloat16),
        value_piece,
        preferred_element_type=jnp.float32,
    )
    weight_sum, summed = (weight_sum, summed)
    attended_heads = (summed / jnp.transpose(weight_sum)[:, :, None]).astype(jnp.bfloat16)
    logsum = jnp.transpose(jnp.log(weight_sum))
    attended = attended_heads.reshape(token_count, H * DH)
    mixed_values = times_right(attended, attention_set[6])
    mixed_factor = rms_factor(mixed_values)
    residual = input_wide + mixed_values * mixed_factor * gain_post
    residual_factor = rms_factor(residual)
    fed_rows = (residual * residual_factor * gain_feed).astype(jnp.bfloat16)
    gate_values = times_right(fed_rows, feedfwd_set[1])
    up_values = times_right(fed_rows, feedfwd_set[2])
    hidden = (gelu_tanh(gate_values) * up_values).astype(jnp.bfloat16)
    down_values = times_right(hidden, feedfwd_set[3])
    down_factor = rms_factor(down_values)
    block_out = (residual + down_values * down_factor * gain_final).astype(jnp.bfloat16)
    feedfwd_back = (
        lax.all_gather(feedfwd_gain, ("seq", "ctx"), axis=0, tiled=True),
        lax.all_gather(gate_weight, ("seq", "ctx"), axis=0, tiled=True),
        lax.all_gather(up_weight, ("seq", "ctx"), axis=0, tiled=True),
        lax.all_gather(down_weight, ("seq", "ctx"), axis=0, tiled=True),
        lax.all_gather(feedfwd_post, ("seq", "ctx"), axis=0, tiled=True),
    )
    cot_wide = cotangent.astype(jnp.float32)
    grad_final = jnp.sum(cot_wide * down_values * down_factor, axis=0)
    down_back = norm_back(down_values, down_factor, gain_final, cot_wide).astype(jnp.bfloat16)
    hidden_back = times_transposed(down_back, feedfwd_back[3])
    gate_back = (hidden_back * up_values * gelu_slope(gate_values)).astype(jnp.bfloat16)
    up_back = (hidden_back * gelu_tanh(gate_values)).astype(jnp.bfloat16)
    fed_back = times_transposed(gate_back, feedfwd_back[1]) + times_transposed(
        up_back, feedfwd_back[2]
    )
    grad_feed = jnp.sum(fed_back * residual * residual_factor, axis=0)
    residual_back = cot_wide + norm_back(residual, residual_factor, gain_feed, fed_back)
    grad_post = jnp.sum(residual_back * mixed_values * mixed_factor, axis=0)
    mixed_back = norm_back(mixed_values, mixed_factor, gain_post, residual_back).astype(
        jnp.bfloat16
    )
    out_share = H * DH // device_total
    down_share = FF // device_total
    column_share = out_share + down_share
    shard_count = column_share * lax.axis_size(("seq", "ctx")) // column_share
    out_term = transposed_times(attended, mixed_back).reshape(shard_count, out_share, D)
    down_term = transposed_times(hidden, down_back).reshape(shard_count, down_share, D)
    column_block = lax.psum_scatter(
        jnp.concatenate([out_term, down_term], axis=1).reshape(
            column_share * lax.axis_size(("seq", "ctx")), D
        ),
        ("seq", "ctx"),
        scatter_dimension=0,
        tiled=True,
    )
    grad_output = column_block[:out_share]
    grad_down = column_block[out_share:]
    attention_back = (
        lax.all_gather(attention_gain, ("seq", "ctx"), axis=0, tiled=True),
        lax.all_gather(query_weight, ("seq", "ctx"), axis=0, tiled=True),
        lax.all_gather(key_weight, ("seq", "ctx"), axis=0, tiled=True),
        lax.all_gather(value_weight, ("seq", "ctx"), axis=0, tiled=True),
        lax.all_gather(query_gain, ("seq", "ctx"), axis=0, tiled=True),
        lax.all_gather(key_gain, ("seq", "ctx"), axis=0, tiled=True),
        lax.all_gather(output_weight, ("seq", "ctx"), axis=0, tiled=True),
        lax.all_gather(attention_post, ("seq", "ctx"), axis=0, tiled=True),
    )
    attended_back = times_transposed(mixed_back, attention_back[6]).reshape(token_count, H, DH)
    key_all, value_all, place_all = (
        lax.all_gather(key_rot, "ctx", axis=0, tiled=True),
        lax.all_gather(value_rows, "ctx", axis=0, tiled=True),
        lax.all_gather(positions, "ctx", axis=0, tiled=True),
    )
    block_len = min(token_count, 128)
    block_count = token_count // block_len

    def back_block(state_now, pieces):
        query_part, place_part, output_part, logsum_part, upper_part = pieces
        query_back, key_back, value_sum = attend_back(
            query_part,
            place_part,
            output_part,
            logsum_part,
            upper_part,
            key_all,
            value_all,
            place_all,
        )
        return ((state_now[0] + key_back, state_now[1] + value_sum), query_back)

    zero_rows = jnp.zeros((key_all.shape[0], DH), jnp.float32)
    blocks_in = (
        query_rot.reshape(block_count, block_len, H, DH),
        positions.reshape(block_count, block_len),
        attended_heads.reshape(block_count, block_len, H, DH),
        logsum.reshape(block_count, block_len, H),
        attended_back.reshape(block_count, block_len, H, DH),
    )
    (key_terms, value_terms), query_parts = lax.scan(back_block, (zero_rows, zero_rows), blocks_in)
    own_rows = lax.psum_scatter(
        jnp.concatenate([key_terms, value_terms], axis=1).astype(jnp.bfloat16),
        "ctx",
        scatter_dimension=0,
        tiled=True,
    ).astype(jnp.float32)
    key_rot_back = own_rows[:, :DH]
    value_back = own_rows[:, DH:].astype(jnp.bfloat16)
    query_rot_back = query_parts.reshape(token_count, H, DH)
    query_up = rotate_back(query_rot_back, cosine[:, None, :], sinus[:, None, :])
    grad_qgain = jnp.sum(query_up * queries * query_factor, axis=(0, 1))
    query_back = (
        norm_back(queries, query_factor, gain_query, query_up)
        .astype(jnp.bfloat16)
        .reshape(token_count, H * DH)
    )
    key_up = rotate_back(key_rot_back, cosine, sinus)
    grad_kgain = jnp.sum(key_up * key_rows * key_factor, axis=0)
    key_back = norm_back(key_rows, key_factor, gain_key, key_up).astype(jnp.bfloat16)
    normed_back = (
        times_transposed(query_back, attention_back[1])
        + times_transposed(key_back, attention_back[2])
        + times_transposed(value_back, attention_back[3])
    )
    grad_attention = jnp.sum(normed_back * input_wide * input_factor, axis=0)
    input_grad = residual_back + norm_back(input_wide, input_factor, gain_attention, normed_back)
    attention_backs = jnp.concatenate([query_back, key_back, value_back], axis=1)
    feedfwd_backs = jnp.concatenate([gate_back, up_back], axis=1)
    row_block = lax.psum_scatter(
        jnp.concatenate(
            [transposed_times(normed, attention_backs), transposed_times(fed_rows, feedfwd_backs)],
            axis=1,
        ),
        ("seq", "ctx"),
        scatter_dimension=0,
        tiled=True,
    )
    grad_query = row_block[:, : H * DH]
    grad_key = row_block[:, H * DH : H * DH + DH]
    grad_value = row_block[:, H * DH + DH : H * DH + 2 * DH]
    grad_gate = row_block[:, H * DH + 2 * DH : H * DH + 2 * DH + FF]
    grad_up = row_block[:, H * DH + 2 * DH + FF :]
    gains_summed = (
        lax.psum_scatter(grad_attention, ("seq", "ctx"), scatter_dimension=0, tiled=True),
        lax.psum_scatter(grad_qgain, ("seq", "ctx"), scatter_dimension=0, tiled=True),
        lax.psum_scatter(grad_kgain, ("seq", "ctx"), scatter_dimension=0, tiled=True),
        lax.psum_scatter(grad_post, ("seq", "ctx"), scatter_dimension=0, tiled=True),
        lax.psum_scatter(grad_feed, ("seq", "ctx"), scatter_dimension=0, tiled=True),
        lax.psum_scatter(grad_final, ("seq", "ctx"), scatter_dimension=0, tiled=True),
    )
    return (
        block_out,
        input_grad,
        gains_summed[0],
        grad_query,
        grad_key,
        grad_value,
        gains_summed[1],
        gains_summed[2],
        grad_output,
        gains_summed[3],
        gains_summed[4],
        grad_gate,
        grad_up,
        grad_down,
        gains_summed[5],
    )


def solution(mesh):
    return jax.shard_map(
        per_device,
        mesh=mesh,
        in_specs=(
            P(("seq", "ctx"), None),
            P(("seq", "ctx")),
            P(("seq", "ctx")),
            P(("seq", "ctx"), None),
            P(("seq", "ctx"), None),
            P(("seq", "ctx"), None),
            P(("seq", "ctx")),
            P(("seq", "ctx")),
            P(("seq", "ctx"), None),
            P(("seq", "ctx")),
            P(("seq", "ctx")),
            P(("seq", "ctx"), None),
            P(("seq", "ctx"), None),
            P(("seq", "ctx"), None),
            P(("seq", "ctx")),
            P(("seq", "ctx"), None),
        ),
        out_specs=(
            P(("seq", "ctx"), None),
            P(("seq", "ctx"), None),
            P(("seq", "ctx")),
            P(("seq", "ctx"), None),
            P(("seq", "ctx"), None),
            P(("seq", "ctx"), None),
            P(("seq", "ctx")),
            P(("seq", "ctx")),
            P(("seq", "ctx"), None),
            P(("seq", "ctx")),
            P(("seq", "ctx")),
            P(("seq", "ctx"), None),
            P(("seq", "ctx"), None),
            P(("seq", "ctx"), None),
            P(("seq", "ctx")),
        ),
        check_vma=False,
    )
```

profile of v0, /device:TPU:0, one launch (start us, length us, event | category | flops | bytes accessed | tf_op | source)
XLA Modules:
  0.0 2184.4 jit_solution(18043881758278048469)
XLA Ops:
  7.3 0.7 all-gather.16.cloned.1.call-update
  8.0 0.7 all-gather.12.cloned.1.call-update
  11.3 0.8 dynamic-update-slice.1
  12.2 0.8 dynamic-update-slice.2
  13.0 0.8 dynamic-update-slice.4
  13.8 0.8 dynamic-update-slice.3
  14.7 0.8 dynamic-update-slice
  15.5 0.8 dynamic-update-slice.5
  16.4 42.4 %all-reduce.16 = (bf16[1152]{0:T(1024)(128)(2,1)S(1)}, bf16[256]{0:T(256)(128)(2,1)S(1)}, bf16[256]{0:T(256)(128)(2,1)S(1)}, bf16[1152]{0:T(1024)(128)(2,1)S(1)}...) all-reduce(bf16[1152]{0:T(1024)(128)(2,1)S(1)} %dynamic-update-slic, ...), channel_id=1, replica_groups=mesh['seq'=4,'ctx'=8] {'seq','ctx'}, use_global_device_ids=true, to_apply=%add | all-reduce | flops 5120 | bytes 20480
  60.6 43.6 %all-gather.2 = bf16[32,36,256]{2,1,0:T(8,128)(2,1)S(1)} all-gather(bf16[1,36,256]{2,1,0:T(8,128)(2,1)} %bitcast.148), channel_id=1, replica_groups=mesh['seq'=4,'ctx'=8] {'seq','ctx'}, dimensions={0}, use_global_device_ids=true | all-gather | bytes 608256 | tf_op jit(solution)/shard_map/all_gather | solution.py:130
  104.4 40.5 %all-gather = bf16[32,36,256]{2,1,0:T(8,128)(2,1)S(1)} all-gather(bf16[1,36,256]{2,1,0:T(8,128)(2,1)S(1)} %bitcast.149), channel_id=1, replica_groups=mesh['seq'=4,'ctx'=8] {'seq','ctx'}, dimensions={0}, use_global_device_ids=true | all-gather | bytes 608256 | tf_op jit(solution)/shard_map/all_gather | solution.py:131
  145.1 10.4 all-gather.1
  158.2 0.9 broadcast_compare_fusion
  159.0 18.2 all_gather.64
  177.5 18.4 all_gather.60
  196.0 2.7 reshape.304
  199.2 1.0 reshape.281
  200.2 1.3 multiply_reduce_fusion.9
  202.0 0.9 copy.162
  203.2 0.9 copy.164
  205.6 0.7 copy-done.69
  206.8 2.4 multiply_reduce_fusion.6
  211.0 45.9 %all-gather.18.cloned.1.call-done = bf16[32,36,6912]{2,1,0:T(8,128)(2,1)} async-done(((bf16[1,36,6912]{2,1,0:T(8,128)(2,1)}), bf16[32,36,6912]{2,1,0:T(8,128)(2,1)}) %all-gather.18.cloned.1.call-update) | async-done | bytes 15925264 | tf_op jit(solution)/shard_map/all_gather | solution.py:139
  256.9 18.5 reshape.306
  275.3 101.3 %all-gather.20.cloned.1.call-done = bf16[32,36,6912]{2,1,0:T(8,128)(2,1)} async-done(((bf16[1,36,6912]{2,1,0:T(8,128)(2,1)}), bf16[32,36,6912]{2,1,0:T(8,128)(2,1)}) %all-gather.20.cloned.1.call-update) | async-done | bytes 15925264 | tf_op jit(solution)/shard_map/all_gather | solution.py:140
  376.6 18.9 reshape.308
  395.5 8.2 fusion.98
  403.8 1.8 copy-done.3
  405.5 1.4 copy-done
  406.9 4.6 multiply_convert_fusion.1
  411.6 76.7 %all-gather.14.cloned.1.call-done = bf16[6912,1152]{1,0:T(8,128)(2,1)} async-done(((bf16[216,1152]{1,0:T(8,128)(2,1)}), bf16[6912,1152]{1,0:T(8,128)(2,1)}) %all-gather.14.cloned.1.call-update) | async-done | bytes 15925264 | tf_op jit(solution)/shard_map/all_gather | solution.py:141
  488.3 8.2 multiply_reduce_fusion.4
  496.5 0.8 fusion.39
  497.3 1.0 fusion.36
  498.3 10.4 multiply_convert_fusion
  508.8 11.2 fusion.99
  520.0 12.6 multiply_reduce_fusion
  532.7 2.3 multiply_reduce_fusion.1
  535.2 0.8 multiply_reduce_fusion.8
  536.0 1.4 fusion.21
  537.4 0.8 fusion.13
  539.0 1.2 fusion.20
  540.2 12.6 fusion.101
  552.8 25.1 %fusion.7 = f32[1152,13824]{1,0:T(8,128)} fusion(bf16[128,1152]{1,0:T(8,128)(2,1)S(1)} %multiply_convert_fusion.2, bf16[128,6912]{1,0:T(8,128)(2,1)} %get-tuple-element.82, bf16[128,6912]{1,0:T(8,128)(2,1)} %copy-done.9), kind=kOutput, calls=%fused_computation.11 | convolution fusion | flops 4083941376 | bytes 67534848 | tf_op jit(solution)/shard_map/dot_general | solution.py:76
  578.0 1.1 pad_maximum_fusion.2
  579.8 0.8 fusion.63
  581.0 24.9 %pad_maximum_fusion.1 = f32[32,248,1152]{2,1,0:T(8,128)} fusion(f32[32,216,1152]{2,1,0:T(8,128)} %bitcast.130, f32[32,32,1152]{2,1,0:T(8,128)S(1)} %fusion.63), kind=kLoop, calls=%fused_computation.1 | loop fusion | flops 9142272 | bytes 73138176 | tf_op jit(solution)/shard_map/concatenate | solution.py:226
  605.9 4.2 reduce-scatter.2.cloned.1.call-done
  610.1 0.9 convert_element_type.115
  611.7 0.8 slice.76
  612.5 4.0 fusion.57
  616.5 47.3 %pad_maximum_fusion = f32[1152,15360]{1,0:T(8,128)} fusion(f32[1152,13824]{1,0:T(8,128)} %fusion.7, f32[1152,1536]{1,0:T(8,128)} %fusion.57), kind=kLoop, calls=%fused_computation | loop fusion | flops 17694720 | bytes 141557760 | tf_op jit(solution)/shard_map/concatenate | solution.py:306
  663.9 1.6 copy-done.2
  665.5 0.9 fusion.100
  666.4 1.5 convolution_add_fusion.1
  667.9 1.6 fusion.48
  669.5 40.2 %all-reduce.14 = (f32[1152]{0:T(1024)S(1)}, f32[256]{0:T(256)S(1)}, f32[256]{0:T(256)S(1)}, f32[1152]{0:T(1024)S(1)}, f32[1152]{0:T(1024)S(1)}, /*index=5*/f32[1152]{0:T(1024)S(1)}) all-reduce(f32[1152]{0:T(1024)S(1)} %get-tuple-element.57, f32[256]{0:T(256)S(1)} %reduce_sum.205, ...), channel_id=3, replica_groups=mesh['seq'=4,'ctx'=8] {'seq','ctx'}, use_global_device_ids=true, to_apply=%region_16.17.clone | all-reduce | flops 5120 | bytes 40960
  713.2 1.1 fusion.45
  714.3 1452.1 %all-reduce.19.cloned.1.call-done = (f32[1152,15360]{1,0:T(8,128)}, f32[7936,1152]{1,0:T(8,128)}) async-done(((f32[1152,15360]{1,0:T(8,128)}, f32[7936,1152]{1,0:T(8,128)}), (f32[1152,15360]{1,0:T(8,128)}, f32[7936,1152]{1,0:T(8,128)})) %all-reduce.19.cloned.1.call-update) | async-done | bytes 107347984
  2166.4 1.6 constant_dynamic-slice_fusion
  2168.0 2.2 constant_dynamic-slice_fusion.2
  2170.3 1.6 constant_dynamic-slice_fusion.1
  2171.9 1.7 fusion.97
  2173.6 3.7 fusion.96
  (221 shorter events, 19.0 us)
Async XLA Ops:
  7.2 137.9 %copy-start.63 = (s32[128]{0:T(128)S(1)}, s32[128]{0:T(128)}, u32[]{:S(2)}) copy-start(s32[128]{0:T(128)} %param.17) | copy-start | bytes 1540
  7.2 97.2 %copy-start.45 = (bf16[36,256]{1,0:T(8,128)(2,1)S(1)}, bf16[36,256]{1,0:T(8,128)(2,1)}, u32[]{:S(2)}) copy-start(bf16[36,256]{1,0:T(8,128)(2,1)} %param.21) | copy-start | bytes 55300
  7.2 148.3 %copy-start.5 = (bf16[128,1152]{1,0:T(8,128)(2,1)S(1)}, bf16[128,1152]{1,0:T(8,128)(2,1)}, u32[]{:S(2)}) copy-start(bf16[128,1152]{1,0:T(8,128)(2,1)} %param.16) | copy-start | bytes 884740
  7.2 188.7 %all-gather.16.cloned.1.call-start = ((), (), s32[]{:S(2)}) async-start(), calls=%async_computation.4 | async-start | bytes 2703360 | tf_op jit(solution)/shard_map/all_gather | solution.py:129
  7.9 198.9 %all-gather.12.cloned.1.call-start = ((), (), s32[]{:S(2)}) async-start(), calls=%async_computation.1 | async-start | bytes 2433024 | tf_op jit(solution)/shard_map/all_gather | solution.py:134
  8.7 248.2 %all-gather.18.cloned.1.call-start = ((), (), s32[]{:S(2)}) async-start(), calls=%async_computation.5 | async-start | bytes 18247680 | tf_op jit(solution)/shard_map/all_gather | solution.py:139
  9.4 367.2 %all-gather.20.cloned.1.call-start = ((), (), s32[]{:S(2)}) async-start(), calls=%async_computation.6 | async-start | bytes 18247680 | tf_op jit(solution)/shard_map/all_gather | solution.py:140
  10.0 478.3 %all-gather.14.cloned.1.call-start = ((), (), s32[]{:S(2)}) async-start(), calls=%async_computation.2 | async-start | bytes 16422912 | tf_op jit(solution)/shard_map/all_gather | solution.py:141
  10.6 599.5 %reduce-scatter.2.cloned.1.call-start = ((), (), s32[]{:S(2)}) async-start(), calls=%async_computation.3 | async-start | bytes 1179648 | tf_op jit(solution)/shard_map/reduce_scatter | solution.py:277
  11.3 166.2 %copy-start.59 = (f32[128]{0:T(128)}, f32[128]{0:T(128)S(1)}, u32[]{:S(2)}) copy-start(f32[128]{0:T(128)S(1)} %convert_element_type.95) | copy-start | bytes 1540
  58.8 98.4 %copy-start.49 = (f32[256]{0:T(256)}, f32[256]{0:T(256)S(1)}, u32[]{:S(2)}) copy-start(f32[256]{0:T(256)S(1)} %convert_element_type.94) | copy-start | bytes 3076
  58.8 145.3 %copy-start.51 = (f32[256]{0:T(256)}, f32[256]{0:T(256)S(1)}, u32[]{:S(2)}) copy-start(f32[256]{0:T(256)S(1)} %convert_element_type.96) | copy-start | bytes 3076
  104.4 91.5 %copy-start.13 = (bf16[1152,256]{1,0:T(8,128)(2,1)}, bf16[1152,256]{1,0:T(8,128)(2,1)S(1)}, u32[]{:S(2)}) copy-start(bf16[1152,256]{1,0:T(8,128)(2,1)S(1)} %reshape.302) | copy-start | bytes 1769476
  145.0 50.9 %copy-start.14 = (bf16[1152,256]{1,0:T(8,128)(2,1)}, bf16[1152,256]{1,0:T(8,128)(2,1)S(1)}, u32[]{:S(2)}) copy-start(bf16[1152,256]{1,0:T(8,128)(2,1)S(1)} %reshape.298) | copy-start | bytes 1769476
  155.5 43.1 %copy-start.61 = (f32[128]{0:T(128)}, f32[128]{0:T(128)S(1)}, u32[]{:S(2)}) copy-start(f32[128]{0:T(128)S(1)} %multiply_power_fusion) | copy-start | bytes 1540
  156.2 42.4 %copy-start.47 = (f32[128]{0:T(128)}, f32[128]{0:T(128)S(1)}, u32[]{:S(2)}) copy-start(f32[128]{0:T(128)S(1)} %get-tuple-element.105) | copy-start | bytes 1540
  156.6 39.3 %copy-start.22 = (f32[128,256]{1,0:T(8,128)}, f32[128,256]{1,0:T(8,128)S(1)}, u32[]{:S(2)}) copy-start(f32[128,256]{1,0:T(8,128)S(1)} %get-tuple-element.115) | copy-start | bytes 393220
  158.2 46.1 %copy-start.26 = (f32[128,128]{1,0:T(8,128)}, f32[128,128]{1,0:T(8,128)S(1)}, u32[]{:S(2)}) copy-start(f32[128,128]{1,0:T(8,128)S(1)} %get-tuple-element.101) | copy-start | bytes 196612
  198.6 4.5 copy-start.1
  201.8 2.5 copy-start.20
  201.8 2.5 copy-start.39
  203.2 3.1 copy-start.29
  204.3 2.5 copy-start.35
  206.8 68.5 %copy-start.15 = (bf16[128,4,256]{0,2,1:T(8,128)(2,1)}, bf16[128,4,256]{0,2,1:T(8,128)(2,1)S(1)}, u32[]{:S(2)}) copy-start(bf16[128,4,256]{0,2,1:T(8,128)(2,1)S(1)} %fusion.23) | copy-start | bytes 786436
  206.8 4.1 copy-start.33
  210.9 64.5 %copy-start.57 = (f32[128]{0:T(128)}, f32[128]{0:T(128)S(1)}, u32[]{:S(2)}) copy-start(f32[128]{0:T(128)S(1)} %get-tuple-element.111) | copy-start | bytes 1540
  395.5 11.4 copy-start
  488.3 8.2 copy-start.12
  488.3 8.2 copy-start.41
  488.3 10.0 copy-start.4
  498.3 10.4 copy-start.24
  508.7 11.2 copy-start.9
  508.7 11.2 copy-start.34
  508.7 11.2 copy-start.58
  520.0 12.7 copy-start.7
  520.0 12.7 copy-start.54
  520.0 12.7 copy-start.67
  520.0 15.0 copy-start.66
  532.6 2.5 copy-start.8
  532.7 2.5 copy-start.16
  532.7 3.3 copy-start.40
  532.7 3.3 copy-start.64
  532.7 3.3 copy-start.70
  535.0 2.4 copy-start.10
  535.2 2.2 copy-start.30
  537.4 2.8 copy-start.25
  552.8 25.1 %copy-start.27 = (f32[128,128]{1,0:T(8,128)S(1)}, f32[128,128]{1,0:T(8,128)}, u32[]{:S(2)}) copy-start(f32[128,128]{1,0:T(8,128)} %copy-done.26) | copy-start | bytes 196612
  552.8 25.2 %copy-start.31 = (bf16[1024,256]{1,0:T(8,128)(2,1)S(1)}, bf16[1024,256]{1,0:T(8,128)(2,1)}, u32[]{:S(2)}) copy-start(bf16[1024,256]{1,0:T(8,128)(2,1)} %fusion.21) | copy-start | bytes 1572868
  552.8 25.2 %copy-start.32 = (bf16[1024,256]{1,0:T(8,128)(2,1)S(1)}, bf16[1024,256]{1,0:T(8,128)(2,1)}, u32[]{:S(2)}) copy-start(bf16[1024,256]{1,0:T(8,128)(2,1)} %fusion.20) | copy-start | bytes 1572868
  578.0 1.8 copy-start.17
  579.1 1587.4 %all-reduce.19.cloned.1.call-start = ((), (), s32[]{:S(2)}) async-start(), calls=%async_computation.7 | async-start | bytes 214695936
  580.9 30.1 %copy-start.60 = (f32[128]{0:T(128)S(1)}, f32[128]{0:T(128)}, u32[]{:S(2)}) copy-start(f32[128]{0:T(128)} %copy-done.59) | copy-start | bytes 1540
  580.9 30.1 %copy-start.62 = (f32[128]{0:T(128)S(1)}, f32[128]{0:T(128)}, u32[]{:S(2)}) copy-start(f32[128]{0:T(128)} %copy-done.61) | copy-start | bytes 1540
  580.9 30.4 %copy-start.23 = (f32[128,256]{1,0:T(8,128)S(1)}, f32[128,256]{1,0:T(8,128)}, u32[]{:S(2)}) copy-start(f32[128,256]{1,0:T(8,128)} %copy-done.22) | copy-start | bytes 393220
  581.0 30.4 %copy-start.50 = (f32[256]{0:T(256)S(1)}, f32[256]{0:T(256)}, u32[]{:S(2)}) copy-start(f32[256]{0:T(256)} %copy-done.49) | copy-start | bytes 3076
  581.0 30.4 %copy-start.56 = (f32[128]{0:T(128)S(1)}, f32[128]{0:T(128)}, u32[]{:S(2)}) copy-start(f32[128]{0:T(128)} %copy-done.55) | copy-start | bytes 1540
  581.0 30.6 %copy-start.65 = (f32[128]{0:T(128)S(1)}, f32[128]{0:T(128)}, u32[]{:S(2)}) copy-start(f32[128]{0:T(128)} %get-tuple-element.106) | copy-start | bytes 1540
  581.0 31.6 %copy-start.48 = (f32[128]{0:T(128)S(1)}, f32[128]{0:T(128)}, u32[]{:S(2)}) copy-start(f32[128]{0:T(128)} %copy-done.47) | copy-start | bytes 1540
  663.8 4.0 copy-start.28
  665.5 4.0 copy-start.42
  665.5 4.0 copy-start.43
  665.5 4.0 copy-start.44
  665.5 47.8 %copy-start.68 = (f32[128]{0:T(128)S(1)}, f32[128]{0:T(128)}, u32[]{:S(2)}) copy-start(f32[128]{0:T(128)} %get-tuple-element.104) | copy-start | bytes 1540
  666.4 46.9 %copy-start.11 = (f32[128,1152]{1,0:T(8,128)S(1)}, f32[128,1152]{1,0:T(8,128)}, u32[]{:S(2)}) copy-start(f32[128,1152]{1,0:T(8,128)} %copy-done.10) | copy-start | bytes 1769476
  (14 other events, 17.7 us)
Sparse Core Ops, SparseCore 0:
  10.9 60.5 all-gather.15
  74.5 56.8 all-gather.11
  134.4 122.4 all-gather.17
  259.7 116.8 all-gather.19
  379.3 108.8 all-gather.13
  579.2 30.8 reduce-scatter.1
  664.0 1502.4 all-reduce.18
where the time goes:
time: 2190 us; the launch traced here: 2180 us
  waiting for transfers between devices  1680 us (77%)
  blocking collectives  214 us (10%)
  matrix products  111 us (5%)
  other arithmetic  88 us (4%)
  local copies, waits for them, and re-layouts  72.5 us (3%)
    unnamed x8, waiting for transfers between devices  1460 us
    all_gather x1, waiting for transfers between devices, per_device(): lax.all_gather(up_weight, ('seq', 'ctx'), axis=0, tiled=True)  101 us
    unnamed x2, blocking collectives  82.6 us
    all_gather x1, waiting for transfers between devices, per_device(): lax.all_gather(down_weight, ('seq', 'ctx'), axis=0, tiled=True)  76.7 us
    unnamed x171, local copies, waits for them, and re-layouts  58.2 us
    concatenate x1, other arithmetic, per_device(): jnp.concatenate([transposed_times(normed, attention_backs), transposed_ti...  47.3 us
    all_gather x1, waiting for transfers between devices, per_device(): lax.all_gather(gate_weight, ('seq', 'ctx'), axis=0, tiled=True)  45.9 us
  transfers between devices with their start and end apart: 7, of which 5 were waited for; matrix products, arithmetic and copies ran while one was open for 5% of the time, Pallas kernels for 0%

commit v1 on v0

--- a/solution.py
+++ b/solution.py
@@ -137,7 +137,12 @@
     feedfwd_set = (
         lax.all_gather(feedfwd_gain, ("seq", "ctx"), axis=0, tiled=True),
         lax.all_gather(gate_weight, ("seq", "ctx"), axis=0, tiled=True),
-        lax.all_gather(up_weight, ("seq", "ctx"), axis=0, tiled=True),
+        jnp.concatenate(
+            lax.all_to_all(
+                jnp.stack([up_weight] * lax.axis_size(("seq", "ctx"))), ("seq", "ctx"), 0, 0
+            ),
+            axis=0,
+        ),
         lax.all_gather(down_weight, ("seq", "ctx"), axis=0, tiled=True),
         lax.all_gather(feedfwd_post, ("seq", "ctx"), axis=0, tiled=True),
     )

time: 2190 us -> 2530 us (1.16)
  blocking collectives: 214 us -> 739 us
  waiting for transfers between devices: 1680 us -> 1460 us
    unnamed x2, blocking collectives: 82.6 us -> 603 us
    all_gather x1, waiting for transfers between devices: 101 us -> 0.01 us  [per_device(): lax.all_gather(up_weight, ('seq', 'ctx'), axis=0, tiled=True)]
    all_gather x1, waiting for transfers between devices: 76.7 us -> 0.01 us  [per_device(): lax.all_gather(down_weight, ('seq', 'ctx'), axis=0, tiled=True)]
    all_gather x1, waiting for transfers between devices: 45.9 us -> 0.02 us  [per_device(): lax.all_gather(gate_weight, ('seq', 'ctx'), axis=0, tiled=True)]
    unnamed x171 -> x187, local copies, waits for them, and re-layouts: 58.2 us -> 55.2 us
  transfers between devices with their start and end apart: 7 -> 8, of which waited for: 5 -> 2; matrix products, arithmetic and copies ran while one was open for 5% -> 6% of each run, Pallas kernels for 0% -> 0%
where the time goes in v1:
time: 2530 us; the launch traced here: 2520 us
  waiting for transfers between devices  1460 us (58%)
  blocking collectives  739 us (29%)
  matrix products  111 us (4%)
  local copies, waits for them, and re-layouts  95.5 us (4%)
  other arithmetic  87.3 us (3%)
    unnamed x8, waiting for transfers between devices  1460 us
    unnamed x2, blocking collectives  603 us
    unnamed x187, local copies, waits for them, and re-layouts  55.2 us
  transfers between devices with their start and end apart: 8, of which 2 were waited for; matrix products, arithmetic and copies ran while one was open for 6% of the time, Pallas kernels for 0%

profile of v1, /device:TPU:0, one launch (start us, length us, event | category | flops | bytes accessed | tf_op | source)
XLA Modules:
  0.0 2516.3 jit_solution(17446173298165265769)
XLA Ops:
  7.2 0.7 all-gather.16.cloned.1.call-update
  8.0 0.7 all-gather.12.cloned.1.call-update
  8.7 0.7 all-gather.18.cloned.1.call-update
  10.0 7.1 stack.2
  17.2 7.4 all-to-all-start
  26.8 562.6 %all-reduce.16 = (bf16[1152]{0:T(1024)(128)(2,1)S(1)}, bf16[256]{0:T(256)(128)(2,1)S(1)}, bf16[256]{0:T(256)(128)(2,1)S(1)}, bf16[1152]{0:T(1024)(128)(2,1)S(1)}...) all-reduce(bf16[1152]{0:T(1024)(128)(2,1)S(1)} %dynamic-update-slic, ...), channel_id=1, replica_groups=mesh['seq'=4,'ctx'=8] {'seq','ctx'}, use_global_device_ids=true, to_apply=%add | all-reduce | flops 5120 | bytes 20480
  589.4 0.6 copy.163
  590.0 0.6 convert_element_type.100
  590.6 0.6 convert_element_type.103
  591.2 46.3 %all-gather.2 = bf16[32,36,256]{2,1,0:T(8,128)(2,1)S(1)} all-gather(bf16[1,36,256]{2,1,0:T(8,128)(2,1)S(1)} %bitcast.148), channel_id=1, replica_groups=mesh['seq'=4,'ctx'=8] {'seq','ctx'}, dimensions={0}, use_global_device_ids=true | all-gather | bytes 608256 | tf_op jit(solution)/shard_map/all_gather | solution.py:130
  637.7 44.5 %all-gather = bf16[32,36,256]{2,1,0:T(8,128)(2,1)S(1)} all-gather(bf16[1,36,256]{2,1,0:T(8,128)(2,1)S(1)} %bitcast.149), channel_id=1, replica_groups=mesh['seq'=4,'ctx'=8] {'seq','ctx'}, dimensions={0}, use_global_device_ids=true | all-gather | bytes 608256 | tf_op jit(solution)/shard_map/all_gather | solution.py:131
  682.4 9.7 all-gather.1
  694.6 0.9 broadcast_compare_fusion
  695.5 17.8 all_gather.63
  713.6 17.5 all_gather.59
  731.1 2.7 reshape.310
  734.3 1.0 reshape.286
  735.4 1.3 multiply_reduce_fusion.9
  737.2 0.9 copy.162
  738.3 0.9 copy.164
  740.1 0.6 log.5
  740.7 0.7 copy-done.77
  741.9 2.4 multiply_reduce_fusion.6
  746.0 18.4 reshape.312
  764.5 18.8 reshape.288
  783.3 8.1 fusion.98
  791.5 1.8 copy-done.3
  793.3 1.3 copy-done
  794.6 4.7 multiply_convert_fusion.1
  799.3 8.2 multiply_reduce_fusion.4
  807.6 0.8 fusion.39
  808.3 1.0 fusion.36
  809.3 10.4 multiply_convert_fusion
  819.7 1.3 copy-done.9
  821.0 11.4 fusion.99
  832.3 18.4 reshape.314
  850.8 12.7 multiply_reduce_fusion
  863.5 2.3 multiply_reduce_fusion.1
  866.0 0.8 multiply_reduce_fusion.8
  866.8 1.4 fusion.21
  868.2 0.8 fusion.13
  869.8 1.2 fusion.20
  871.1 12.6 fusion.101
  883.6 25.1 fusion.7
  908.8 1.1 pad_maximum_fusion.2
  910.7 0.8 fusion.63
  911.8 25.0 pad_maximum_fusion.1
  936.8 5.0 reduce-scatter.2.cloned.1.call-done
  941.8 0.9 convert_element_type.115
  943.4 0.8 slice.76
  944.2 4.0 fusion.57
  948.2 47.2 %pad_maximum_fusion = f32[1152,15360]{1,0:T(8,128)} fusion(f32[1152,13824]{1,0:T(8,128)} %fusion.7, f32[1152,1536]{1,0:T(8,128)} %fusion.57), kind=kLoop, calls=%fused_computation | loop fusion | flops 17694720 | bytes 141557760 | tf_op jit(solution)/shard_map/concatenate | solution.py:311
  995.6 1.6 copy-done.2
  997.2 0.9 fusion.100
  998.1 1.5 convolution_add_fusion.1
  999.5 1.7 fusion.48
  1001.2 40.3 %all-reduce.14 = (f32[1152]{0:T(1024)S(1)}, f32[256]{0:T(256)S(1)}, f32[256]{0:T(256)S(1)}, f32[1152]{0:T(1024)S(1)}, f32[1152]{0:T(1024)S(1)}, /*index=5*/f32[1152]{0:T(1024)S(1)}) all-reduce(f32[1152]{0:T(1024)S(1)} %get-tuple-element.57, f32[256]{0:T(256)S(1)} %reduce_sum.205, ...), channel_id=3, replica_groups=mesh['seq'=4,'ctx'=8] {'seq','ctx'}, use_global_device_ids=true, to_apply=%region_16.17.clone | all-reduce | flops 5120 | bytes 40960
  1045.1 1.1 fusion.45
  1046.2 1452.2 %all-reduce.19.cloned.1.call-done = (f32[1152,15360]{1,0:T(8,128)}, f32[7936,1152]{1,0:T(8,128)}) async-done(((f32[1152,15360]{1,0:T(8,128)}, f32[7936,1152]{1,0:T(8,128)}), (f32[1152,15360]{1,0:T(8,128)}, f32[7936,1152]{1,0:T(8,128)})) %all-reduce.19.cloned.1.call-update) | async-done | bytes 107347984
  2498.3 1.6 constant_dynamic-slice_fusion
  2499.9 2.2 constant_dynamic-slice_fusion.2
  2502.2 1.6 constant_dynamic-slice_fusion.1
  2503.8 1.7 fusion.97
  2505.5 3.7 fusion.96
  (241 shorter events, 16.6 us)
Async XLA Ops:
  7.2 723.9 %all-gather.16.cloned.1.call-start = ((), (), s32[]{:S(2)}) async-start(), calls=%async_computation.5 | async-start | bytes 2703360 | tf_op jit(solution)/shard_map/all_gather | solution.py:129
  7.9 734.0 %all-gather.12.cloned.1.call-start = ((), (), s32[]{:S(2)}) async-start(), calls=%async_computation.2 | async-start | bytes 2433024 | tf_op jit(solution)/shard_map/all_gather | solution.py:134
  8.7 737.4 %all-gather.18.cloned.1.call-start = ((), (), s32[]{:S(2)}) async-start(), calls=%async_computation.6 | async-start | bytes 18247680 | tf_op jit(solution)/shard_map/all_gather | solution.py:139
  9.4 789.9 %all-gather.14.cloned.1.call-start = ((), (), s32[]{:S(2)}) async-start(), calls=%async_computation.3 | async-start | bytes 16422912 | tf_op jit(solution)/shard_map/all_gather | solution.py:146
  17.1 8.2 copy-start.65
  17.1 8.2 copy-start.71
  17.1 8.5 copy-start.72
  17.1 8.7 copy-start.73
  17.1 9.0 copy-start.74
  17.1 9.2 copy-start.75
  17.1 9.5 copy-start.76
  17.2 574.1 %copy-start.46 = (bf16[36,256]{1,0:T(8,128)(2,1)S(1)}, bf16[36,256]{1,0:T(8,128)(2,1)}, u32[]{:S(2)}) copy-start(bf16[36,256]{1,0:T(8,128)(2,1)} %param.20) | copy-start | bytes 55300
  17.2 620.5 %copy-start.47 = (bf16[36,256]{1,0:T(8,128)(2,1)S(1)}, bf16[36,256]{1,0:T(8,128)(2,1)}, u32[]{:S(2)}) copy-start(bf16[36,256]{1,0:T(8,128)(2,1)} %param.21) | copy-start | bytes 55300
  17.2 747.3 %all-to-all-start = ((bf16[32,36,6912]{2,1,0:T(8,128)(2,1)}), bf16[32,36,6912]{2,1,0:T(8,128)(2,1)}, u32[]{:S(2)}, u32[]{:S(2)}) async-start(bf16[32,36,6912]{2,1,0:T(8,128)(2,1)} %stack.2), calls=%async_computation | async-start | bytes 35389440 | tf_op jit(solution)/shard_map/all_to_all | solution.py:141
  24.6 667.4 %copy-start.5 = (bf16[128,1152]{1,0:T(8,128)(2,1)S(1)}, bf16[128,1152]{1,0:T(8,128)(2,1)}, u32[]{:S(2)}) copy-start(bf16[128,1152]{1,0:T(8,128)(2,1)} %param.16) | copy-start | bytes 884740
  24.6 807.7 %all-gather.20.cloned.1.call-start = ((), (), s32[]{:S(2)}) async-start(), calls=%async_computation.7 | async-start | bytes 18247680 | tf_op jit(solution)/shard_map/all_gather | solution.py:205
  25.2 916.6 %reduce-scatter.2.cloned.1.call-start = ((), (), s32[]{:S(2)}) async-start(), calls=%async_computation.4 | async-start | bytes 1179648 | tf_op jit(solution)/shard_map/reduce_scatter | solution.py:282
  25.3 688.2 %copy-start.61 = (f32[128]{0:T(128)}, f32[128]{0:T(128)S(1)}, u32[]{:S(2)}) copy-start(f32[128]{0:T(128)S(1)} %convert_element_type.95) | copy-start | bytes 1540
  589.4 104.3 %copy-start.51 = (f32[256]{0:T(256)}, f32[256]{0:T(256)S(1)}, u32[]{:S(2)}) copy-start(f32[256]{0:T(256)S(1)} %convert_element_type.94) | copy-start | bytes 3076
  589.4 149.8 %copy-start.53 = (f32[256]{0:T(256)}, f32[256]{0:T(256)S(1)}, u32[]{:S(2)}) copy-start(f32[256]{0:T(256)S(1)} %convert_element_type.96) | copy-start | bytes 3076
  637.7 93.3 %copy-start.14 = (bf16[1152,256]{1,0:T(8,128)(2,1)}, bf16[1152,256]{1,0:T(8,128)(2,1)S(1)}, u32[]{:S(2)}) copy-start(bf16[1152,256]{1,0:T(8,128)(2,1)S(1)} %reshape.308) | copy-start | bytes 1769476
  682.4 48.7 %copy-start.15 = (bf16[1152,256]{1,0:T(8,128)(2,1)}, bf16[1152,256]{1,0:T(8,128)(2,1)S(1)}, u32[]{:S(2)}) copy-start(bf16[1152,256]{1,0:T(8,128)(2,1)S(1)} %reshape.304) | copy-start | bytes 1769476
  692.1 41.7 %copy-start.63 = (f32[128]{0:T(128)}, f32[128]{0:T(128)S(1)}, u32[]{:S(2)}) copy-start(f32[128]{0:T(128)S(1)} %multiply_power_fusion) | copy-start | bytes 1540
  692.8 41.0 %copy-start.49 = (f32[128]{0:T(128)}, f32[128]{0:T(128)S(1)}, u32[]{:S(2)}) copy-start(f32[128]{0:T(128)S(1)} %get-tuple-element.105) | copy-start | bytes 1540
  693.1 37.9 %copy-start.23 = (f32[128,256]{1,0:T(8,128)}, f32[128,256]{1,0:T(8,128)S(1)}, u32[]{:S(2)}) copy-start(f32[128,256]{1,0:T(8,128)S(1)} %get-tuple-element.115) | copy-start | bytes 393220
  694.6 44.7 %copy-start.27 = (f32[128,128]{1,0:T(8,128)}, f32[128,128]{1,0:T(8,128)S(1)}, u32[]{:S(2)}) copy-start(f32[128,128]{1,0:T(8,128)S(1)} %get-tuple-element.101) | copy-start | bytes 196612
  733.7 4.5 copy-start.1
  738.3 3.1 copy-start.30
  741.9 22.6 copy-start.16
  741.9 4.0 copy-start.34
  745.9 18.6 copy-start.59
  783.3 11.3 copy-start
  799.3 8.2 copy-start.12
  799.3 8.2 copy-start.42
  799.3 10.0 copy-start.4
  809.3 10.4 copy-start.25
  850.7 12.7 copy-start.7
  850.7 12.7 copy-start.13
  850.7 12.7 copy-start.35
  850.7 12.7 copy-start.56
  850.7 12.7 copy-start.60
  850.7 12.7 copy-start.69
  850.8 15.1 copy-start.68
  863.5 3.3 copy-start.41
  863.5 3.3 copy-start.66
  863.5 3.3 copy-start.78
  868.2 2.8 copy-start.26
  883.6 25.1 copy-start.28
  883.6 25.2 copy-start.32
  883.6 25.2 %copy-start.33 = (bf16[1024,256]{1,0:T(8,128)(2,1)S(1)}, bf16[1024,256]{1,0:T(8,128)(2,1)}, u32[]{:S(2)}) copy-start(bf16[1024,256]{1,0:T(8,128)(2,1)} %fusion.20) | copy-start | bytes 1572868
  909.9 1588.4 %all-reduce.19.cloned.1.call-start = ((), (), s32[]{:S(2)}) async-start(), calls=%async_computation.8 | async-start | bytes 214695936
  911.7 31.0 %copy-start.62 = (f32[128]{0:T(128)S(1)}, f32[128]{0:T(128)}, u32[]{:S(2)}) copy-start(f32[128]{0:T(128)} %copy-done.61) | copy-start | bytes 1540
  911.8 31.0 %copy-start.64 = (f32[128]{0:T(128)S(1)}, f32[128]{0:T(128)}, u32[]{:S(2)}) copy-start(f32[128]{0:T(128)} %copy-done.63) | copy-start | bytes 1540
  911.8 31.3 %copy-start.24 = (f32[128,256]{1,0:T(8,128)S(1)}, f32[128,256]{1,0:T(8,128)}, u32[]{:S(2)}) copy-start(f32[128,256]{1,0:T(8,128)} %copy-done.23) | copy-start | bytes 393220
  911.8 31.3 %copy-start.52 = (f32[256]{0:T(256)S(1)}, f32[256]{0:T(256)}, u32[]{:S(2)}) copy-start(f32[256]{0:T(256)} %copy-done.51) | copy-start | bytes 3076
  911.8 31.3 %copy-start.58 = (f32[128]{0:T(128)S(1)}, f32[128]{0:T(128)}, u32[]{:S(2)}) copy-start(f32[128]{0:T(128)} %copy-done.57) | copy-start | bytes 1540
  911.8 31.5 %copy-start.67 = (f32[128]{0:T(128)S(1)}, f32[128]{0:T(128)}, u32[]{:S(2)}) copy-start(f32[128]{0:T(128)} %get-tuple-element.106) | copy-start | bytes 1540
  911.8 32.4 %copy-start.50 = (f32[128]{0:T(128)S(1)}, f32[128]{0:T(128)}, u32[]{:S(2)}) copy-start(f32[128]{0:T(128)} %copy-done.49) | copy-start | bytes 1540
  995.5 4.0 copy-start.29
  997.2 4.0 copy-start.43
  997.2 4.1 copy-start.44
  997.2 4.1 copy-start.45
  997.2 47.9 %copy-start.70 = (f32[128]{0:T(128)S(1)}, f32[128]{0:T(128)}, u32[]{:S(2)}) copy-start(f32[128]{0:T(128)} %get-tuple-element.104) | copy-start | bytes 1540
  998.0 47.0 %copy-start.11 = (f32[128,1152]{1,0:T(8,128)S(1)}, f32[128,1152]{1,0:T(8,128)}, u32[]{:S(2)}) copy-start(f32[128,1152]{1,0:T(8,128)} %copy-done.10) | copy-start | bytes 1769476
  (23 other events, 37.9 us)
Sparse Core Ops, SparseCore 0:
  10.8 129.4 all-gather.15
  143.3 126.4 all-gather.11
  272.8 187.4 all-gather.17
  463.0 128.8 all-gather.13
  594.8 128.8 all-gather.19
  910.0 31.7 reduce-scatter.1
  995.6 1502.6 all-reduce.18
